TPU v7x, 32 devices: a whole 2x2x4 slice. The times are simulated.
32 devices in a mesh: grp: 2 (over y), ja: 4 (over z), ia: 4 (over x, core).
Axes of the slice: x: 2, y: 2, z: 4, core: 2. Of those that a mesh axis runs over, the one named last changes fastest.
Arguments:
- pos_vel: float32 [6, 8192], P(None, ('grp', 'ja')), parts along dimension 1, may hold values from -6 to 6
- acc_jerk: float32 [6, 8192], P(None, ('grp', 'ja')), parts along dimension 1, may hold values from -6 to 6
- mass: float32 [8192], P(('grp', 'ja')), parts along dimension 0, may hold values from 7.324219e-05 to 0.0007324219
- age: float32 [8192], P(('grp', 'ja')), parts along dimension 0, may hold values from 0.125 to 0.5
- active_local: int32 [12288], P(('grp', 'ia')), parts along dimension 0, may hold values from 0 to 1023
- active_owner: int32 [12288], P(('grp', 'ia')), parts along dimension 0, may hold values from 0 to 3
Outputs:
- state: float32 [6, 12288], P(None, ('grp', 'ia')), parts along dimension 1
- forces: float32 [7, 12288], P(None, ('grp', 'ia')), parts along dimension 1
There are 2 independent parts, one for each index of `grp`. A program takes and returns all parts, laid end to end along the dimension named above; each array names one. Nothing has to cross between parts.
All inputs are finite; a program needn't handle non-finite values.
Results may differ from a plain program's by a relative error of at most 0.0003.
Values sent between devices are 32-bit elements; how exact they have to be, the bound alone decides.
No kernel may reach another device: no remote copies, remote signals or barrier semaphores. Data moves between devices by JAX's collectives and lax.ppermute only.
A program may use at most 64 MiB of HBM per device.

v0:
```python
import jax
import jax.numpy as jnp
from jax import lax
from jax.sharding import PartitionSpec as P

soften = 0.0004


def predict(pos_vel, acc_jerk, age):
    position = pos_vel[0:3]
    velocity = pos_vel[3:6]
    accel = acc_jerk[0:3]
    jolt = acc_jerk[3:6]
    step_len = age[None, :]
    new_pos = position + step_len * (velocity + step_len * (accel * 0.5 + step_len * jolt / 6.0))
    new_vel = velocity + step_len * (accel + step_len * jolt * 0.5)
    return jnp.concatenate([new_pos, new_vel], axis=0)


def pair_terms(targets, sources, masses):
    delta_pos = sources[0:3, :, None] - targets[0:3, None, :]
    delta_vel = sources[3:6, :, None] - targets[3:6, None, :]
    dist_sq = jnp.sum(delta_pos * delta_pos, axis=0) + soften
    inverse = lax.rsqrt(dist_sq)
    inv_sq = inverse * inverse
    weighted = masses[:, None] * inverse
    weighted_cube = weighted * inv_sq
    radial = 3.0 * jnp.sum(delta_pos * delta_vel, axis=0) * inv_sq
    accel = jnp.sum(weighted_cube[None] * delta_pos, axis=1)
    jolt = jnp.sum(weighted_cube[None] * (delta_vel - radial[None] * delta_pos), axis=1)
    potential = -jnp.sum(weighted, axis=0)
    return jnp.concatenate([accel, jolt, potential[None]], axis=0)


def block_terms(targets, sources, masses):
    count = targets.shape[1]
    width = min(512, count)
    nblocks = count // width
    src_count = sources.shape[1]
    src_width = min(512, src_count)
    src_blocks = src_count // src_width
    source_pieces = sources.reshape(6, src_blocks, src_width).transpose(1, 0, 2)
    mass_pieces = masses.reshape(src_blocks, src_width)
    pieces = targets.reshape(6, nblocks, width).transpose(1, 0, 2)

    def one_block(piece):

        def accumulate(total, parts):
            return (total + pair_terms(piece, parts[0], parts[1]), None)

        total, unused = lax.scan(
            accumulate, jnp.zeros((7, width), jnp.float32), (source_pieces, mass_pieces)
        )
        return total

    results = lax.map(one_block, pieces)
    return results.transpose(1, 0, 2).reshape(7, count)


def correct(history, forces):
    pred_pos = history[0:3]
    pred_vel = history[3:6]
    old_acc = history[6:9]
    old_jolt = history[9:12]
    step_len = history[12:13]
    new_acc = forces[0:3]
    new_jolt = forces[3:6]
    differ = old_acc - new_acc
    square = step_len * step_len
    cubed = square * step_len
    fourth = square * square
    fifth = fourth * step_len
    second = (-6.0 * differ - step_len * (4.0 * old_jolt + 2.0 * new_jolt)) / square
    third = (12.0 * differ + 6.0 * step_len * (old_jolt + new_jolt)) / cubed
    position = pred_pos + fourth / 24.0 * second + fifth / 120.0 * third
    velocity = pred_vel + cubed / 6.0 * second + fourth / 24.0 * third
    return jnp.concatenate([position, velocity], axis=0)


def local(pos_vel, acc_jerk, mass, age, active_local, active_owner):
    shard_rank = lax.axis_index("ja")
    predicted = predict(pos_vel, acc_jerk, age)
    stacked = jnp.concatenate([predicted, acc_jerk, age[None, :]], axis=0)
    picked = jnp.take(stacked, active_local, axis=1)
    owned = active_owner == shard_rank
    contrib = jnp.where(owned[None, :], picked, 0.0)
    history = lax.psum(contrib, "ja")
    partial_value = block_terms(history[0:6], predicted, mass)
    forces = lax.psum(partial_value, "ja")
    state = correct(history, forces)
    return (state, forces)


def solution(mesh):
    return jax.shard_map(
        local,
        mesh=mesh,
        in_specs=(
            P(None, ("grp", "ja")),
            P(None, ("grp", "ja")),
            P(("grp", "ja")),
            P(("grp", "ja")),
            P(("grp", "ia")),
            P(("grp", "ia")),
        ),
        out_specs=(P(None, ("grp", "ia")), P(None, ("grp", "ia"))),
        check_vma=False,
    )
```

profile of v0, /device:TPU:0, one launch (start us, length us, event | category | flops | bytes accessed | tf_op | source)
XLA Modules:
  0.0 92.8 jit_solution(16712219660879244907)
XLA Ops:
  7.2 0.7 compare_select_fusion
  7.9 0.9 multiply_add_fusion.1
  8.8 0.8 pad_maximum_fusion
  9.9 2.6 %gather_fusion = f32[1536,13]{1,0:T(8,128)S(1)} fusion(f32[13,1024]{0,1:T(8,128)S(1)} %copy.93, s32[2048]{0:T(1024)S(1)} %pad_clamp_fusion), kind=kCustom, calls=%fused_computation | custom fusion | bytes 165888 | tf_op jit(solution)/shard_map/jit(_take)/gather | solution.py:84
  12.5 0.3 copy.94
  12.8 0.7 select_bitcast_fusion
  13.5 37.3 %all-reduce.2.cloned.1.call-done = f32[13,1536]{1,0:T(8,128)} async-done(((f32[13,1536]{1,0:T(8,128)}), f32[13,1536]{1,0:T(8,128)}) %all-reduce.2.cloned.1.call-update) | async-done | bytes 79888 | tf_op jit(solution)/shard_map/psum | solution.py:87
  50.8 0.8 slice.71
  51.6 15.3 %while.22 = (s32[]{:T(128)}, f32[3,7,512]{2,1,0:T(8,128)S(1)}, f32[3,6,512]{2,1,0:T(8,128)S(1)}, f32[2,512]{1,0:T(2,128)S(1)}, f32[2,6,512]{2,1,0:T(8,128)S(1)},...) while((s32[]{:T(128)}, f32[3,7,512]{2,1,0:T(8,128)S(1)}, f32[3,6,512]{2,1,0:T(8,128)S(1)}, ...), condition=%wide.region_9.10_spmd, body=%wide.region_1.9_spmd.sunk | while | flops 12332038 | bytes 8612156 | solution.py:56
  51.6 5.1 %while.23 = (s32[]{:T(128)}, f32[7,512]{1,0:T(8,128)S(1)}, f32[2,512]{1,0:T(2,128)S(1)}, f32[2,6,512]{2,1,0:T(8,128)S(1)}, f32[6,512]{1,0:T(8,128)S(1)}, /*index=5*/s32[]{:T(128)}, s32[]{:T(128)}, s32[]{}) while((s32[]{:T(128)}, f32[7,512]{1,0:T(8,128)S(1)}, f32[2,512]{1,0:T(2,128)S(1)}, f32[2,6,512]{2,1,0:T(8,128)S(1)}, ...), condition=%wide.region_8.8_spmd.clone, body=%wide.region_2.7_spmd.clone.sunk | while | flops 12332036 | bytes 8554623 | solution.py:51
  51.7 1.0 %fusion.13 = (f32[512,512]{1,0:T(8,128)S(1)}, f32[512,512]{1,0:T(8,128)S(1)}) fusion(f32[3,512]{1,0:T(4,128)S(1)} %get-tuple-element.214, f32[3,512]{1,0:T(4,128)S(1)} %get-tuple-element.215, f32[3,512]{1,0:T(4,128)S(1)} %get-tuple-element.216, f32[3,512]{1,0:T(4,128)S(1)} %get-tuple-element.217), kind=kLoop, calls=%fused_computation.10.clone.1 | loop fusion | flops 4194304 | bytes 2121728 | tf_op jit(solution)/shard_map/while/body/eval_jaxpr/while/body/eval_jaxpr/reduce_sum | solution.py:28
  52.6 0.3 multiply_multiply_fusion.5
  53.0 1.1 %fusion.14 = (f32[3,512]{1,0:T(4,128)S(1)}, f32[3,512]{1,0:T(4,128)S(1)}) fusion(f32[512,512]{1,0:T(8,128)S(1)} %get-tuple-element.221, f32[3,512]{1,0:T(4,128)S(1)} %get-tuple-element.216, f32[3,512]{1,0:T(4,128)S(1)} %get-tuple-element.217, f32[512,512]{1,0:T(8,128)S(1)} %get-tuple-element.222, f32[3,512]{1,0:T(4,128)S(1)} %get-tuple-element.214, ...), kind=kLoop, calls=%fused_computation.9.clone.1 | loop fusion | flops 6288384 | bytes 2134016 | tf_op jit(solution)/shard_map/while/body/eval_jaxpr/while/body/eval_jaxpr/reduce_sum | solution.py:29
  54.2 1.0 %fusion.13 = (f32[512,512]{1,0:T(8,128)S(1)}, f32[512,512]{1,0:T(8,128)S(1)}) fusion(f32[3,512]{1,0:T(4,128)S(1)} %get-tuple-element.214, f32[3,512]{1,0:T(4,128)S(1)} %get-tuple-element.215, f32[3,512]{1,0:T(4,128)S(1)} %get-tuple-element.216, f32[3,512]{1,0:T(4,128)S(1)} %get-tuple-element.217), kind=kLoop, calls=%fused_computation.10.clone.1 | loop fusion | flops 4194304 | bytes 2121728 | tf_op jit(solution)/shard_map/while/body/eval_jaxpr/while/body/eval_jaxpr/reduce_sum | solution.py:28
  55.2 0.3 multiply_multiply_fusion.5
  55.5 1.1 %fusion.14 = (f32[3,512]{1,0:T(4,128)S(1)}, f32[3,512]{1,0:T(4,128)S(1)}) fusion(f32[512,512]{1,0:T(8,128)S(1)} %get-tuple-element.221, f32[3,512]{1,0:T(4,128)S(1)} %get-tuple-element.216, f32[3,512]{1,0:T(4,128)S(1)} %get-tuple-element.217, f32[512,512]{1,0:T(8,128)S(1)} %get-tuple-element.222, f32[3,512]{1,0:T(4,128)S(1)} %get-tuple-element.214, ...), kind=kLoop, calls=%fused_computation.9.clone.1 | loop fusion | flops 6288384 | bytes 2134016 | tf_op jit(solution)/shard_map/while/body/eval_jaxpr/while/body/eval_jaxpr/reduce_sum | solution.py:29
  56.7 5.1 %while.23 = (s32[]{:T(128)}, f32[7,512]{1,0:T(8,128)S(1)}, f32[2,512]{1,0:T(2,128)S(1)}, f32[2,6,512]{2,1,0:T(8,128)S(1)}, f32[6,512]{1,0:T(8,128)S(1)}, /*index=5*/s32[]{:T(128)}, s32[]{:T(128)}, s32[]{}) while((s32[]{:T(128)}, f32[7,512]{1,0:T(8,128)S(1)}, f32[2,512]{1,0:T(2,128)S(1)}, f32[2,6,512]{2,1,0:T(8,128)S(1)}, ...), condition=%wide.region_8.8_spmd.clone, body=%wide.region_2.7_spmd.clone.sunk | while | flops 12332036 | bytes 8554623 | solution.py:51
  56.8 1.0 %fusion.13 = (f32[512,512]{1,0:T(8,128)S(1)}, f32[512,512]{1,0:T(8,128)S(1)}) fusion(f32[3,512]{1,0:T(4,128)S(1)} %get-tuple-element.214, f32[3,512]{1,0:T(4,128)S(1)} %get-tuple-element.215, f32[3,512]{1,0:T(4,128)S(1)} %get-tuple-element.216, f32[3,512]{1,0:T(4,128)S(1)} %get-tuple-element.217), kind=kLoop, calls=%fused_computation.10.clone.1 | loop fusion | flops 4194304 | bytes 2121728 | tf_op jit(solution)/shard_map/while/body/eval_jaxpr/while/body/eval_jaxpr/reduce_sum | solution.py:28
  57.8 0.3 multiply_multiply_fusion.5
  58.1 1.1 %fusion.14 = (f32[3,512]{1,0:T(4,128)S(1)}, f32[3,512]{1,0:T(4,128)S(1)}) fusion(f32[512,512]{1,0:T(8,128)S(1)} %get-tuple-element.221, f32[3,512]{1,0:T(4,128)S(1)} %get-tuple-element.216, f32[3,512]{1,0:T(4,128)S(1)} %get-tuple-element.217, f32[512,512]{1,0:T(8,128)S(1)} %get-tuple-element.222, f32[3,512]{1,0:T(4,128)S(1)} %get-tuple-element.214, ...), kind=kLoop, calls=%fused_computation.9.clone.1 | loop fusion | flops 6288384 | bytes 2134016 | tf_op jit(solution)/shard_map/while/body/eval_jaxpr/while/body/eval_jaxpr/reduce_sum | solution.py:29
  59.3 1.0 %fusion.13 = (f32[512,512]{1,0:T(8,128)S(1)}, f32[512,512]{1,0:T(8,128)S(1)}) fusion(f32[3,512]{1,0:T(4,128)S(1)} %get-tuple-element.214, f32[3,512]{1,0:T(4,128)S(1)} %get-tuple-element.215, f32[3,512]{1,0:T(4,128)S(1)} %get-tuple-element.216, f32[3,512]{1,0:T(4,128)S(1)} %get-tuple-element.217), kind=kLoop, calls=%fused_computation.10.clone.1 | loop fusion | flops 4194304 | bytes 2121728 | tf_op jit(solution)/shard_map/while/body/eval_jaxpr/while/body/eval_jaxpr/reduce_sum | solution.py:28
  60.3 0.3 multiply_multiply_fusion.5
  60.6 1.1 %fusion.14 = (f32[3,512]{1,0:T(4,128)S(1)}, f32[3,512]{1,0:T(4,128)S(1)}) fusion(f32[512,512]{1,0:T(8,128)S(1)} %get-tuple-element.221, f32[3,512]{1,0:T(4,128)S(1)} %get-tuple-element.216, f32[3,512]{1,0:T(4,128)S(1)} %get-tuple-element.217, f32[512,512]{1,0:T(8,128)S(1)} %get-tuple-element.222, f32[3,512]{1,0:T(4,128)S(1)} %get-tuple-element.214, ...), kind=kLoop, calls=%fused_computation.9.clone.1 | loop fusion | flops 6288384 | bytes 2134016 | tf_op jit(solution)/shard_map/while/body/eval_jaxpr/while/body/eval_jaxpr/reduce_sum | solution.py:29
  61.8 5.1 %while.23 = (s32[]{:T(128)}, f32[7,512]{1,0:T(8,128)S(1)}, f32[2,512]{1,0:T(2,128)S(1)}, f32[2,6,512]{2,1,0:T(8,128)S(1)}, f32[6,512]{1,0:T(8,128)S(1)}, /*index=5*/s32[]{:T(128)}, s32[]{:T(128)}, s32[]{}) while((s32[]{:T(128)}, f32[7,512]{1,0:T(8,128)S(1)}, f32[2,512]{1,0:T(2,128)S(1)}, f32[2,6,512]{2,1,0:T(8,128)S(1)}, ...), condition=%wide.region_8.8_spmd.clone, body=%wide.region_2.7_spmd.clone.sunk | while | flops 12332036 | bytes 8554623 | solution.py:51
  61.9 1.0 %fusion.13 = (f32[512,512]{1,0:T(8,128)S(1)}, f32[512,512]{1,0:T(8,128)S(1)}) fusion(f32[3,512]{1,0:T(4,128)S(1)} %get-tuple-element.214, f32[3,512]{1,0:T(4,128)S(1)} %get-tuple-element.215, f32[3,512]{1,0:T(4,128)S(1)} %get-tuple-element.216, f32[3,512]{1,0:T(4,128)S(1)} %get-tuple-element.217), kind=kLoop, calls=%fused_computation.10.clone.1 | loop fusion | flops 4194304 | bytes 2121728 | tf_op jit(solution)/shard_map/while/body/eval_jaxpr/while/body/eval_jaxpr/reduce_sum | solution.py:28
  62.9 0.3 multiply_multiply_fusion.5
  63.2 1.1 %fusion.14 = (f32[3,512]{1,0:T(4,128)S(1)}, f32[3,512]{1,0:T(4,128)S(1)}) fusion(f32[512,512]{1,0:T(8,128)S(1)} %get-tuple-element.221, f32[3,512]{1,0:T(4,128)S(1)} %get-tuple-element.216, f32[3,512]{1,0:T(4,128)S(1)} %get-tuple-element.217, f32[512,512]{1,0:T(8,128)S(1)} %get-tuple-element.222, f32[3,512]{1,0:T(4,128)S(1)} %get-tuple-element.214, ...), kind=kLoop, calls=%fused_computation.9.clone.1 | loop fusion | flops 6288384 | bytes 2134016 | tf_op jit(solution)/shard_map/while/body/eval_jaxpr/while/body/eval_jaxpr/reduce_sum | solution.py:29
  64.4 1.0 %fusion.13 = (f32[512,512]{1,0:T(8,128)S(1)}, f32[512,512]{1,0:T(8,128)S(1)}) fusion(f32[3,512]{1,0:T(4,128)S(1)} %get-tuple-element.214, f32[3,512]{1,0:T(4,128)S(1)} %get-tuple-element.215, f32[3,512]{1,0:T(4,128)S(1)} %get-tuple-element.216, f32[3,512]{1,0:T(4,128)S(1)} %get-tuple-element.217), kind=kLoop, calls=%fused_computation.10.clone.1 | loop fusion | flops 4194304 | bytes 2121728 | tf_op jit(solution)/shard_map/while/body/eval_jaxpr/while/body/eval_jaxpr/reduce_sum | solution.py:28
  65.4 0.3 multiply_multiply_fusion.5
  65.7 1.1 %fusion.14 = (f32[3,512]{1,0:T(4,128)S(1)}, f32[3,512]{1,0:T(4,128)S(1)}) fusion(f32[512,512]{1,0:T(8,128)S(1)} %get-tuple-element.221, f32[3,512]{1,0:T(4,128)S(1)} %get-tuple-element.216, f32[3,512]{1,0:T(4,128)S(1)} %get-tuple-element.217, f32[512,512]{1,0:T(8,128)S(1)} %get-tuple-element.222, f32[3,512]{1,0:T(4,128)S(1)} %get-tuple-element.214, ...), kind=kLoop, calls=%fused_computation.9.clone.1 | loop fusion | flops 6288384 | bytes 2134016 | tf_op jit(solution)/shard_map/while/body/eval_jaxpr/while/body/eval_jaxpr/reduce_sum | solution.py:29
  66.9 18.2 %psum.15 = f32[7,1536]{1,0:T(8,128)S(1)} all-reduce(f32[7,1536]{1,0:T(8,128)S(1)} %bitcast.36), channel_id=1, replica_groups=mesh['grp'=2,'ja'=4,'ia'=4] {'ja'}, use_global_device_ids=true, to_apply=%region_10.11 | all-reduce | flops 10752 | bytes 86016 | tf_op jit(solution)/shard_map/psum | solution.py:89
  85.3 0.6 pad_maximum_fusion.1
  (60 shorter events, 0.9 us)
Async XLA Ops:
  7.2 43.6 %all-reduce.2.cloned.1.call-start = ((), (), s32[]{:S(2)}) async-start(), calls=%async_computation | async-start | bytes 196608 | tf_op jit(solution)/shard_map/psum | solution.py:87
  9.6 3.1 %copy-start.2 = (s32[1536]{0:T(1024)S(1)}, s32[1536]{0:T(1024)}, u32[]{:S(2)}) copy-start(s32[1536]{0:T(1024)} %param.14) | copy-start | bytes 18436
  9.6 3.1 %copy-start.3 = (s32[1536]{0:T(1024)S(1)}, s32[1536]{0:T(1024)}, u32[]{:S(2)}) copy-start(s32[1536]{0:T(1024)} %param.15) | copy-start | bytes 18436
  9.8 3.6 %copy-start.4 = (f32[1024]{0:T(1024)S(1)}, f32[1024]{0:T(1024)}, u32[]{:S(2)}) copy-start(f32[1024]{0:T(1024)} %param.12) | copy-start | bytes 12292
  51.6 33.5 %copy-start = (f32[13,1536]{1,0:T(8,128)S(1)}, f32[13,1536]{1,0:T(8,128)}, u32[]{:S(2)}) copy-start(f32[13,1536]{1,0:T(8,128)} %all-reduce.2.cloned.1.call-done) | copy-start | bytes 239620
  85.1 0.9 copy-start.1
Sparse Core Ops, SparseCore 0:
  13.5 37.1 all-reduce.1
where the time goes:
time: 93.2 us; the launch traced here: 92.8 us
  waiting for transfers between devices  37.3 us (40%)
  other arithmetic  18.5 us (20%)
  blocking collectives  18.2 us (20%)
  between operations  14.2 us (15%)
  local copies, waits for them, and re-layouts  4.12 us (4%)
    psum x1, waiting for transfers between devices, local(): history = lax.psum(contrib, 'ja')  37.3 us
    psum x1, blocking collectives, local(): forces = lax.psum(partial_value, 'ja')  18.2 us
    reduce_sum x6, other arithmetic, pair_terms(): accel = jnp.sum(weighted_cube[None] * delta_pos, axis=1)  6.74 us
    reduce_sum x6, other arithmetic, pair_terms(): radial = 3.0 * jnp.sum(delta_pos * delta_vel, axis=0) * inv_sq  5.85 us
    gather x2, local copies, waits for them, and re-layouts, local(): picked = jnp.take(stacked, active_local, axis=1)  2.86 us
  transfers between devices with their start and end apart: 1, of which 1 were waited for; matrix products, arithmetic and copies ran while one was open for 0% of the time, Pallas kernels for 0%

commit v1 on v0

--- a/solution.py
+++ b/solution.py
@@ -86,7 +86,9 @@
     contrib = jnp.where(owned[None, :], picked, 0.0)
     history = lax.psum(contrib, "ja")
     partial_value = block_terms(history[0:6], predicted, mass)
-    forces = lax.psum(partial_value, "ja")
+    forces = partial_value
+    for hop in (1, 2):
+        forces = forces + lax.ppermute(forces, "ja", [(dev, dev ^ hop) for dev in range(4)])
     state = correct(history, forces)
     return (state, forces)
 

time: 93.2 us -> 84 us (0.901)
  blocking collectives: 18.2 us -> 0 us
  waiting for transfers between devices: 37.3 us -> 42.3 us
  starting transfers between devices: 0.04 us -> 4.1 us
    psum x1 -> x0, blocking collectives: 18.2 us -> none  [local(): forces = lax.psum(partial_value, 'ja')]
    ppermute x0 -> x2, waiting for transfers between devices: none -> 5.02 us  [local(): lax.ppermute(forces, 'ja', [(dev, dev ^ hop) for dev in range(4)])]
    ppermute x0 -> x2, starting transfers between devices: none -> 4.06 us  [local(): lax.ppermute(forces, 'ja', [(dev, dev ^ hop) for dev in range(4)])]
  transfers between devices with their start and end apart: 1 -> 3, of which waited for: 1 -> 3; matrix products, arithmetic and copies ran while one was open for 0% -> 0% of each run, Pallas kernels for 0% -> 0%
where the time goes in v1:
time: 84 us; the launch traced here: 83.7 us
  waiting for transfers between devices  42.3 us (50%)
  other arithmetic  18.4 us (22%)
  between operations  14.1 us (17%)
  local copies, waits for them, and re-layouts  4.12 us (5%)
  starting transfers between devices  4.1 us (5%)
    psum x1, waiting for transfers between devices, local(): history = lax.psum(contrib, 'ja')  37.3 us
    reduce_sum x6, other arithmetic, pair_terms(): accel = jnp.sum(weighted_cube[None] * delta_pos, axis=1)  6.69 us
    reduce_sum x6, other arithmetic, pair_terms(): radial = 3.0 * jnp.sum(delta_pos * delta_vel, axis=0) * inv_sq  5.78 us
    ppermute x2, waiting for transfers between devices, local(): lax.ppermute(forces, 'ja', [(dev, dev ^ hop) for dev in range(4)])  5.02 us
    ppermute x2, starting transfers between devices, local(): lax.ppermute(forces, 'ja', [(dev, dev ^ hop) for dev in range(4)])  4.06 us
    gather x2, local copies, waits for them, and re-layouts, local(): picked = jnp.take(stacked, active_local, axis=1)  2.86 us
    mul x6, other arithmetic, pair_terms(): weighted_cube = weighted * inv_sq  1.86 us
  transfers between devices with their start and end apart: 3, of which 3 were waited for; matrix products, arithmetic and copies ran while one was open for 0% of the time, Pallas kernels for 0%

profile of v1, /device:TPU:0, one launch (start us, length us, event | category | flops | bytes accessed | tf_op | source)
XLA Modules:
  0.0 83.7 jit_solution(17084433539700668973)
XLA Ops:
  7.2 0.9 %multiply_add_fusion.1 = (f32[3,1024]{1,0:T(4,128)S(1)}, f32[3,1024]{1,0:T(4,128)S(1)}) fusion(f32[6,1024]{1,0:T(8,128)} %param.10, f32[6,1024]{1,0:T(8,128)} %param.11, f32[1024]{0:T(1024)} %param.13), kind=kLoop, calls=%fused_computation.34 | loop fusion | flops 36864 | bytes 77824 | tf_op jit(solution)/shard_map/add | solution.py:15
  8.1 0.8 pad_maximum_fusion
  9.1 0.8 compare_select_fusion
  9.9 2.6 %gather_fusion = f32[1536,13]{1,0:T(8,128)S(1)} fusion(f32[13,1024]{0,1:T(8,128)S(1)} %copy.101, s32[2048]{0:T(1024)S(1)} %pad_clamp_fusion), kind=kCustom, calls=%fused_computation | custom fusion | bytes 165888 | tf_op jit(solution)/shard_map/jit(_take)/gather | solution.py:84
  12.8 0.7 select_bitcast_fusion
  13.5 37.3 %all-reduce.2.cloned.1.call-done = f32[13,1536]{1,0:T(8,128)} async-done(((f32[13,1536]{1,0:T(8,128)}), f32[13,1536]{1,0:T(8,128)}) %all-reduce.2.cloned.1.call-update) | async-done | bytes 79888 | tf_op jit(solution)/shard_map/psum | solution.py:87
  50.8 0.8 slice.71
  51.6 15.2 %while.22 = (s32[]{:T(128)}, f32[3,7,512]{2,1,0:T(8,128)S(1)}, f32[3,6,512]{2,1,0:T(8,128)S(1)}, f32[2,512]{1,0:T(2,128)S(1)}, f32[2,6,512]{2,1,0:T(8,128)S(1)},...) while((s32[]{:T(128)}, f32[3,7,512]{2,1,0:T(8,128)S(1)}, f32[3,6,512]{2,1,0:T(8,128)S(1)}, ...), condition=%wide.region_9.10_spmd, body=%wide.region_1.9_spmd.sunk | while | flops 12332038 | bytes 8612140 | solution.py:56
  51.6 5.0 %while.23 = (s32[]{:T(128)}, f32[7,512]{1,0:T(8,128)S(1)}, f32[2,512]{1,0:T(2,128)S(1)}, f32[2,6,512]{2,1,0:T(8,128)S(1)}, f32[6,512]{1,0:T(8,128)S(1)}, /*index=5*/s32[]{:T(128)}, s32[]{:T(128)}, s32[]{}) while((s32[]{:T(128)}, f32[7,512]{1,0:T(8,128)S(1)}, f32[2,512]{1,0:T(2,128)S(1)}, f32[2,6,512]{2,1,0:T(8,128)S(1)}, ...), condition=%wide.region_8.8_spmd.clone, body=%wide.region_2.7_spmd.clone.sunk | while | flops 12332036 | bytes 8554615 | solution.py:51
  51.7 1.0 %fusion.13 = (f32[512,512]{1,0:T(8,128)S(1)}, f32[512,512]{1,0:T(8,128)S(1)}) fusion(f32[3,512]{1,0:T(4,128)S(1)} %get-tuple-element.214, f32[3,512]{1,0:T(4,128)S(1)} %get-tuple-element.215, f32[3,512]{1,0:T(4,128)S(1)} %get-tuple-element.216, f32[3,512]{1,0:T(4,128)S(1)} %get-tuple-element.217), kind=kLoop, calls=%fused_computation.10.clone.1 | loop fusion | flops 4194304 | bytes 2121728 | tf_op jit(solution)/shard_map/while/body/eval_jaxpr/while/body/eval_jaxpr/reduce_sum | solution.py:28
  52.7 0.3 multiply_multiply_fusion.5
  53.0 1.1 %fusion.14 = (f32[3,512]{1,0:T(4,128)S(1)}, f32[3,512]{1,0:T(4,128)S(1)}) fusion(f32[512,512]{1,0:T(8,128)S(1)} %get-tuple-element.221, f32[3,512]{1,0:T(4,128)S(1)} %get-tuple-element.216, f32[3,512]{1,0:T(4,128)S(1)} %get-tuple-element.217, f32[512,512]{1,0:T(8,128)S(1)} %get-tuple-element.222, f32[3,512]{1,0:T(4,128)S(1)} %get-tuple-element.214, ...), kind=kLoop, calls=%fused_computation.9.clone.1 | loop fusion | flops 6288384 | bytes 2134016 | tf_op jit(solution)/shard_map/while/body/eval_jaxpr/while/body/eval_jaxpr/reduce_sum | solution.py:29
  54.2 1.0 %fusion.13 = (f32[512,512]{1,0:T(8,128)S(1)}, f32[512,512]{1,0:T(8,128)S(1)}) fusion(f32[3,512]{1,0:T(4,128)S(1)} %get-tuple-element.214, f32[3,512]{1,0:T(4,128)S(1)} %get-tuple-element.215, f32[3,512]{1,0:T(4,128)S(1)} %get-tuple-element.216, f32[3,512]{1,0:T(4,128)S(1)} %get-tuple-element.217), kind=kLoop, calls=%fused_computation.10.clone.1 | loop fusion | flops 4194304 | bytes 2121728 | tf_op jit(solution)/shard_map/while/body/eval_jaxpr/while/body/eval_jaxpr/reduce_sum | solution.py:28
  55.2 0.3 multiply_multiply_fusion.5
  55.5 1.1 %fusion.14 = (f32[3,512]{1,0:T(4,128)S(1)}, f32[3,512]{1,0:T(4,128)S(1)}) fusion(f32[512,512]{1,0:T(8,128)S(1)} %get-tuple-element.221, f32[3,512]{1,0:T(4,128)S(1)} %get-tuple-element.216, f32[3,512]{1,0:T(4,128)S(1)} %get-tuple-element.217, f32[512,512]{1,0:T(8,128)S(1)} %get-tuple-element.222, f32[3,512]{1,0:T(4,128)S(1)} %get-tuple-element.214, ...), kind=kLoop, calls=%fused_computation.9.clone.1 | loop fusion | flops 6288384 | bytes 2134016 | tf_op jit(solution)/shard_map/while/body/eval_jaxpr/while/body/eval_jaxpr/reduce_sum | solution.py:29
  56.7 5.0 %while.23 = (s32[]{:T(128)}, f32[7,512]{1,0:T(8,128)S(1)}, f32[2,512]{1,0:T(2,128)S(1)}, f32[2,6,512]{2,1,0:T(8,128)S(1)}, f32[6,512]{1,0:T(8,128)S(1)}, /*index=5*/s32[]{:T(128)}, s32[]{:T(128)}, s32[]{}) while((s32[]{:T(128)}, f32[7,512]{1,0:T(8,128)S(1)}, f32[2,512]{1,0:T(2,128)S(1)}, f32[2,6,512]{2,1,0:T(8,128)S(1)}, ...), condition=%wide.region_8.8_spmd.clone, body=%wide.region_2.7_spmd.clone.sunk | while | flops 12332036 | bytes 8554615 | solution.py:51
  56.8 1.0 %fusion.13 = (f32[512,512]{1,0:T(8,128)S(1)}, f32[512,512]{1,0:T(8,128)S(1)}) fusion(f32[3,512]{1,0:T(4,128)S(1)} %get-tuple-element.214, f32[3,512]{1,0:T(4,128)S(1)} %get-tuple-element.215, f32[3,512]{1,0:T(4,128)S(1)} %get-tuple-element.216, f32[3,512]{1,0:T(4,128)S(1)} %get-tuple-element.217), kind=kLoop, calls=%fused_computation.10.clone.1 | loop fusion | flops 4194304 | bytes 2121728 | tf_op jit(solution)/shard_map/while/body/eval_jaxpr/while/body/eval_jaxpr/reduce_sum | solution.py:28
  57.8 0.3 multiply_multiply_fusion.5
  58.1 1.1 %fusion.14 = (f32[3,512]{1,0:T(4,128)S(1)}, f32[3,512]{1,0:T(4,128)S(1)}) fusion(f32[512,512]{1,0:T(8,128)S(1)} %get-tuple-element.221, f32[3,512]{1,0:T(4,128)S(1)} %get-tuple-element.216, f32[3,512]{1,0:T(4,128)S(1)} %get-tuple-element.217, f32[512,512]{1,0:T(8,128)S(1)} %get-tuple-element.222, f32[3,512]{1,0:T(4,128)S(1)} %get-tuple-element.214, ...), kind=kLoop, calls=%fused_computation.9.clone.1 | loop fusion | flops 6288384 | bytes 2134016 | tf_op jit(solution)/shard_map/while/body/eval_jaxpr/while/body/eval_jaxpr/reduce_sum | solution.py:29
  59.3 1.0 %fusion.13 = (f32[512,512]{1,0:T(8,128)S(1)}, f32[512,512]{1,0:T(8,128)S(1)}) fusion(f32[3,512]{1,0:T(4,128)S(1)} %get-tuple-element.214, f32[3,512]{1,0:T(4,128)S(1)} %get-tuple-element.215, f32[3,512]{1,0:T(4,128)S(1)} %get-tuple-element.216, f32[3,512]{1,0:T(4,128)S(1)} %get-tuple-element.217), kind=kLoop, calls=%fused_computation.10.clone.1 | loop fusion | flops 4194304 | bytes 2121728 | tf_op jit(solution)/shard_map/while/body/eval_jaxpr/while/body/eval_jaxpr/reduce_sum | solution.py:28
  60.3 0.3 multiply_multiply_fusion.5
  60.6 1.1 %fusion.14 = (f32[3,512]{1,0:T(4,128)S(1)}, f32[3,512]{1,0:T(4,128)S(1)}) fusion(f32[512,512]{1,0:T(8,128)S(1)} %get-tuple-element.221, f32[3,512]{1,0:T(4,128)S(1)} %get-tuple-element.216, f32[3,512]{1,0:T(4,128)S(1)} %get-tuple-element.217, f32[512,512]{1,0:T(8,128)S(1)} %get-tuple-element.222, f32[3,512]{1,0:T(4,128)S(1)} %get-tuple-element.214, ...), kind=kLoop, calls=%fused_computation.9.clone.1 | loop fusion | flops 6288384 | bytes 2134016 | tf_op jit(solution)/shard_map/while/body/eval_jaxpr/while/body/eval_jaxpr/reduce_sum | solution.py:29
  61.8 5.0 %while.23 = (s32[]{:T(128)}, f32[7,512]{1,0:T(8,128)S(1)}, f32[2,512]{1,0:T(2,128)S(1)}, f32[2,6,512]{2,1,0:T(8,128)S(1)}, f32[6,512]{1,0:T(8,128)S(1)}, /*index=5*/s32[]{:T(128)}, s32[]{:T(128)}, s32[]{}) while((s32[]{:T(128)}, f32[7,512]{1,0:T(8,128)S(1)}, f32[2,512]{1,0:T(2,128)S(1)}, f32[2,6,512]{2,1,0:T(8,128)S(1)}, ...), condition=%wide.region_8.8_spmd.clone, body=%wide.region_2.7_spmd.clone.sunk | while | flops 12332036 | bytes 8554615 | solution.py:51
  61.9 1.0 %fusion.13 = (f32[512,512]{1,0:T(8,128)S(1)}, f32[512,512]{1,0:T(8,128)S(1)}) fusion(f32[3,512]{1,0:T(4,128)S(1)} %get-tuple-element.214, f32[3,512]{1,0:T(4,128)S(1)} %get-tuple-element.215, f32[3,512]{1,0:T(4,128)S(1)} %get-tuple-element.216, f32[3,512]{1,0:T(4,128)S(1)} %get-tuple-element.217), kind=kLoop, calls=%fused_computation.10.clone.1 | loop fusion | flops 4194304 | bytes 2121728 | tf_op jit(solution)/shard_map/while/body/eval_jaxpr/while/body/eval_jaxpr/reduce_sum | solution.py:28
  63.2 1.1 %fusion.14 = (f32[3,512]{1,0:T(4,128)S(1)}, f32[3,512]{1,0:T(4,128)S(1)}) fusion(f32[512,512]{1,0:T(8,128)S(1)} %get-tuple-element.221, f32[3,512]{1,0:T(4,128)S(1)} %get-tuple-element.216, f32[3,512]{1,0:T(4,128)S(1)} %get-tuple-element.217, f32[512,512]{1,0:T(8,128)S(1)} %get-tuple-element.222, f32[3,512]{1,0:T(4,128)S(1)} %get-tuple-element.214, ...), kind=kLoop, calls=%fused_computation.9.clone.1 | loop fusion | flops 6288384 | bytes 2134016 | tf_op jit(solution)/shard_map/while/body/eval_jaxpr/while/body/eval_jaxpr/reduce_sum | solution.py:29
  64.4 1.0 %fusion.13 = (f32[512,512]{1,0:T(8,128)S(1)}, f32[512,512]{1,0:T(8,128)S(1)}) fusion(f32[3,512]{1,0:T(4,128)S(1)} %get-tuple-element.214, f32[3,512]{1,0:T(4,128)S(1)} %get-tuple-element.215, f32[3,512]{1,0:T(4,128)S(1)} %get-tuple-element.216, f32[3,512]{1,0:T(4,128)S(1)} %get-tuple-element.217), kind=kLoop, calls=%fused_computation.10.clone.1 | loop fusion | flops 4194304 | bytes 2121728 | tf_op jit(solution)/shard_map/while/body/eval_jaxpr/while/body/eval_jaxpr/reduce_sum | solution.py:28
  65.7 1.1 %fusion.14 = (f32[3,512]{1,0:T(4,128)S(1)}, f32[3,512]{1,0:T(4,128)S(1)}) fusion(f32[512,512]{1,0:T(8,128)S(1)} %get-tuple-element.221, f32[3,512]{1,0:T(4,128)S(1)} %get-tuple-element.216, f32[3,512]{1,0:T(4,128)S(1)} %get-tuple-element.217, f32[512,512]{1,0:T(8,128)S(1)} %get-tuple-element.222, f32[3,512]{1,0:T(4,128)S(1)} %get-tuple-element.214, ...), kind=kLoop, calls=%fused_computation.9.clone.1 | loop fusion | flops 6288384 | bytes 2134016 | tf_op jit(solution)/shard_map/while/body/eval_jaxpr/while/body/eval_jaxpr/reduce_sum | solution.py:29
  66.9 1.5 %collective-permute-start = (f32[7,1536]{1,0:T(8,128)S(1)}, f32[7,1536]{1,0:T(8,128)S(1)}, u32[]{:S(2)}, u32[]{:S(2)}) collective-permute-start(f32[7,1536]{1,0:T(8,128)S(1)} %bitcast.36), channel_id=1, source_target_pairs={{0,4},{4,0},{8,12},{12,8},{1,5},{5,1},{9,13},{13,9},{2,6},{6,2},{1... | collective-permute-start | bytes 129032 | tf_op jit(solution)/shard_map/ppermute | solution.py:91
  68.4 2.7 %collective-permute-done = f32[7,1536]{1,0:T(8,128)S(1)} collective-permute-done((f32[7,1536]{1,0:T(8,128)S(1)}, f32[7,1536]{1,0:T(8,128)S(1)}, u32[]{:S(2)}, u32[]{:S(2)}) %collective-permute-start) | collective-permute-done | bytes 43040 | tf_op jit(solution)/shard_map/ppermute | solution.py:91
  71.0 2.6 %collective-permute-start.1 = (f32[7,1536]{1,0:T(8,128)S(1)}, f32[7,1536]{1,0:T(8,128)S(1)}, u32[]{:S(2)}, u32[]{:S(2)}) collective-permute-start(f32[7,1536]{1,0:T(8,128)S(1)} %add.78), channel_id=1, source_target_pairs={{0,8},{4,12},{8,0},{12,4},{1,9},{5,13},{9,1},{13,5},{2,10},{6,14},... | collective-permute-start | bytes 129032 | tf_op jit(solution)/shard_map/ppermute | solution.py:91
  73.7 2.4 %collective-permute-done.1 = f32[7,1536]{1,0:T(8,128)S(1)} collective-permute-done((f32[7,1536]{1,0:T(8,128)S(1)}, f32[7,1536]{1,0:T(8,128)S(1)}, u32[]{:S(2)}, u32[]{:S(2)}) %collective-permute-start.1) | collective-permute-done | bytes 43040 | tf_op jit(solution)/shard_map/ppermute | solution.py:91
  76.2 0.6 pad_maximum_fusion.1
  (65 shorter events, 1.8 us)
Async XLA Ops:
  7.2 43.7 %all-reduce.2.cloned.1.call-start = ((), (), s32[]{:S(2)}) async-start(), calls=%async_computation | async-start | bytes 196608 | tf_op jit(solution)/shard_map/psum | solution.py:87
  9.1 3.7 %copy-start.2 = (s32[1536]{0:T(1024)S(1)}, s32[1536]{0:T(1024)}, u32[]{:S(2)}) copy-start(s32[1536]{0:T(1024)} %param.14) | copy-start | bytes 18436
  9.1 3.7 %copy-start.3 = (s32[1536]{0:T(1024)S(1)}, s32[1536]{0:T(1024)}, u32[]{:S(2)}) copy-start(s32[1536]{0:T(1024)} %param.15) | copy-start | bytes 18436
  9.9 3.6 %copy-start.4 = (f32[1024]{0:T(1024)S(1)}, f32[1024]{0:T(1024)}, u32[]{:S(2)}) copy-start(f32[1024]{0:T(1024)} %param.12) | copy-start | bytes 12292
  51.6 22.0 %copy-start = (f32[13,1536]{1,0:T(8,128)S(1)}, f32[13,1536]{1,0:T(8,128)}, u32[]{:S(2)}) copy-start(f32[13,1536]{1,0:T(8,128)} %all-reduce.2.cloned.1.call-done) | copy-start | bytes 239620
  66.9 4.2 %collective-permute-start = (f32[7,1536]{1,0:T(8,128)S(1)}, f32[7,1536]{1,0:T(8,128)S(1)}, u32[]{:S(2)}, u32[]{:S(2)}) collective-permute-start(f32[7,1536]{1,0:T(8,128)S(1)} %bitcast.36), channel_id=1, source_target_pairs={{0,4},{4,0},{8,12},{12,8},{1,5},{5,1},{9,13},{13,9},{2,6},{6,2},{1... | collective-permute-start | bytes 129032 | tf_op jit(solution)/shard_map/ppermute | solution.py:91
  71.0 5.0 %collective-permute-start.1 = (f32[7,1536]{1,0:T(8,128)S(1)}, f32[7,1536]{1,0:T(8,128)S(1)}, u32[]{:S(2)}, u32[]{:S(2)}) collective-permute-start(f32[7,1536]{1,0:T(8,128)S(1)} %add.78), channel_id=1, source_target_pairs={{0,8},{4,12},{8,0},{12,4},{1,9},{5,13},{9,1},{13,5},{2,10},{6,14},... | collective-permute-start | bytes 129032 | tf_op jit(solution)/shard_map/ppermute | solution.py:91
  76.1 0.7 copy-start.1
Sparse Core Ops, SparseCore 0:
  13.6 37.1 all-reduce.1
